TPU v7x, 32 devices: a whole 2x2x4 slice. The times are simulated.
32 devices in a mesh: img: 2 (over core), band: 4 (over z), pw: 4 (over y, x).
Axes of the slice: x: 2, y: 2, z: 4, core: 2. Of those that a mesh axis runs over, the one named last changes fastest.
Arguments:
- coefficients: bfloat16 [2, 1024, 32, 2048], P('img', None, ('band', 'pw')), may hold values from -6 to 6
- rotation: bfloat16 [2, 1024, 256], P('img'), may hold values from -0.1875 to 0.1875
- positions: int32 [2, 3, 256], P('img'), may hold values from 0 to 63, as said below
- start_pos: int32 [3, 256], replicated, may hold values from 0 to 63, as said below
- end_pos: int32 [3, 256], replicated, may hold values from 0 to 63, as said below
- species: int32 [256], replicated, may hold values from 0 to 3
- depth: float32 [4], replicated, may hold values from 0.5 to 3
Outputs:
- correction: bfloat16 [2, 256, 32, 2048], P('img', None, ('band', 'pw'))
- ritz_values: float32 [2, 256], P('img')
- band_force: float32 [2, 3, 256], P('img')
- along_force: float32 [2], P('img')
Inputs may be any that keep to these rules, and one draw needn't show every extreme that they name: `positions`: grid index of each atom's centre along each dimension. `start_pos`: grid index of each atom's centre along each dimension. `end_pos`: grid index of each atom's centre along each dimension.
All inputs are finite; a program needn't handle non-finite values.
Results may differ from a plain program's by a relative error of at most 0.012.
The roundings to bfloat16 on the way count: a program that leaves them out, or rounds other values in their place, can miss the bound.
Values may be sent and summed in bfloat16 or wider, within the bound.
A program may use at most 128 MiB of HBM per device.

v0:
```python
import math
import jax
import jax.numpy as jnp
from jax import lax
from jax.sharding import PartitionSpec as P

G = 64
W = 32
BANDS = 1024
BLOCK = 256
SPECIES = 4
kinetic_scale = 0.01
sigma_cells = 3.0
spring_constant = 2.0
epsilon = 1e-06
highest = lax.Precision.HIGHEST


def passed_along(block, axis, distance):
    devices = range(lax.axis_size(axis))
    route = [(i - distance, i) for i in devices if i - distance in devices]
    return lax.ppermute(block, axis, route)


def phases(box_order, box_size, grid_size):
    wavenum = box_order - box_size // 2
    grid_cells = jnp.arange(grid_size, dtype=jnp.int32)
    turn_count = jnp.mod(wavenum[:, None] * grid_cells[None, :], grid_size)
    return turn_count.astype(jnp.float32) * (2.0 * math.pi / grid_size)


def forward_table(box_order, box_size, grid_size):
    angle_tab = phases(box_order, box_size, grid_size)
    cosine = jnp.cos(angle_tab) / math.sqrt(box_size)
    sine_part = jnp.sin(angle_tab) / math.sqrt(box_size)
    dft_table = jnp.stack(
        [jnp.stack([cosine, sine_part], 1), jnp.stack([-sine_part, cosine], 1)], 0
    )
    return dft_table.astype(jnp.bfloat16)


def inverse_table(box_order, box_size, grid_size):
    angle_tab = phases(box_order, box_size, grid_size).T
    factor = math.sqrt(box_size) / grid_size
    cosine = jnp.cos(angle_tab) * factor
    sine_part = jnp.sin(angle_tab) * factor
    dft_table = jnp.stack(
        [jnp.stack([cosine, -sine_part], 1), jnp.stack([sine_part, cosine], 1)], 0
    )
    return dft_table.astype(jnp.bfloat16)


def section_zy(coeff_block, table_z, table_y):
    leading = coeff_block.shape[0]
    planes = coeff_block.shape[1]
    split_up = coeff_block.reshape(leading, planes, W, 2, W)
    along_z = jnp.einsum(
        "blyck,ckdn->blydn", split_up, table_z, preferred_element_type=jnp.float32
    ).astype(jnp.bfloat16)
    along_y = jnp.einsum(
        "blycz,cydm->blmdz", along_z, table_y, preferred_element_type=jnp.float32
    ).astype(jnp.bfloat16)
    return along_y.reshape(leading, planes, G * 2 * G)


def section_x(arrived, table_x):
    leading = arrived.shape[0]
    y_rows = arrived.shape[2] // (2 * G)
    split_up = arrived.reshape(leading, W, y_rows, 2, G)
    return jnp.einsum("bxycz,cxdn->bnydz", split_up, table_x, preferred_element_type=jnp.float32)


def section_x_inverse(weighted, table_x):
    leading = weighted.shape[0]
    y_rows = weighted.shape[2]
    along_x = jnp.einsum(
        "bnydz,dncx->bxycz", weighted, table_x, preferred_element_type=jnp.float32
    ).astype(jnp.bfloat16)
    return along_x.reshape(leading, W, y_rows * 2 * G)


def section_zy_inverse(returned, table_y, table_z):
    leading = returned.shape[0]
    planes = returned.shape[1]
    split_up = returned.reshape(leading, planes, G, 2, G)
    along_y = jnp.einsum(
        "blmdz,dmcy->blycz", split_up, table_y, preferred_element_type=jnp.float32
    ).astype(jnp.bfloat16)
    along_z = jnp.einsum("blydn,dnck->blyck", along_y, table_z, preferred_element_type=jnp.float32)
    return along_z.reshape(leading, planes, W * 2 * W)


def wrap_offset(values):
    return jnp.mod(values + G // 2, G) - G // 2


def gaussians(coords, grid_cells):
    offset = wrap_offset(grid_cells[None, :] - coords[:, None]).astype(jnp.float32)
    return (jnp.exp(-offset * offset / (2.0 * sigma_cells * sigma_cells)), offset)


def atom_tables(own_pos, y_cells):
    grid_cells = jnp.arange(G, dtype=jnp.int32)
    gauss_x, offset_x = gaussians(own_pos[0], grid_cells)
    gauss_y, offset_y = gaussians(own_pos[1], y_cells)
    gauss_z, offset_z = gaussians(own_pos[2], grid_cells)
    return (gauss_x, offset_x, gauss_y, offset_y, gauss_z, offset_z)


def local_potential(tables, strength):
    gauss_x, offset_x, gauss_y, offset_y, gauss_z, offset_z = tables
    atom_count = gauss_x.shape[0]
    joined = (gauss_y[:, :, None] * gauss_z[:, None, :]).reshape(atom_count, -1)
    potential = jnp.dot((strength[:, None] * gauss_x).T, joined, precision=highest)
    return (potential, joined)


def atom_forces(density, tables, joined, strength):
    gauss_x, offset_x, gauss_y, offset_y, gauss_z, offset_z = tables
    atom_count = gauss_x.shape[0]
    with_y = ((gauss_y * offset_y)[:, :, None] * gauss_z[:, None, :]).reshape(atom_count, -1)
    with_z = (gauss_y[:, :, None] * (gauss_z * offset_z)[:, None, :]).reshape(atom_count, -1)
    stacked = jnp.concatenate([joined, with_y, with_z], 0)
    moments = jnp.dot(density, stacked.T, precision=highest)
    prefactor = -strength / (sigma_cells * sigma_cells)
    force_x = prefactor * jnp.sum(gauss_x * offset_x * moments[:, :atom_count].T, 1)
    force_y = prefactor * jnp.sum(gauss_x * moments[:, atom_count : 2 * atom_count].T, 1)
    force_z = prefactor * jnp.sum(gauss_x * moments[:, 2 * atom_count :].T, 1)
    return jnp.stack([force_x, force_y, force_z], 0)


def space_work(in_space, own_pos, strength, y_rows):
    y_cells = jnp.arange(y_rows, dtype=jnp.int32)
    tables = atom_tables(own_pos, y_cells)
    potential, joined = local_potential(tables, strength)
    grid_potential = potential.reshape(G, y_rows, G)
    density = jnp.sum(in_space * in_space, axis=(0, 3)).reshape(G, y_rows * G) / BLOCK
    force_part = atom_forces(density, tables, joined, strength)
    weighted = (in_space * grid_potential[:, :, None, :]).astype(jnp.bfloat16)
    return (weighted, force_part)


def kinetic_table(x_cells):
    entries = jnp.arange(W * 2 * W, dtype=jnp.int32)
    wave_y = entries // (2 * W) - W // 2
    wave_z = jnp.mod(entries, W) - W // 2
    wave_x = x_cells - W // 2
    squared = wave_x[:, None] * wave_x[:, None] + (wave_y * wave_y + wave_z * wave_z)[None, :]
    return kinetic_scale * 0.5 * squared.astype(jnp.float32)


def rotate_quarter(values):
    leading = values.shape[0]
    middle = values.shape[1]
    split_up = values.reshape(leading, middle, W, 2, W)
    turned = jnp.stack([-split_up[:, :, :, 1, :], split_up[:, :, :, 0, :]], 3)
    return turned.reshape(values.shape)


def chain_forces(force, own_pos, before, after):
    ahead_step = wrap_offset(after - own_pos).astype(jnp.float32)
    behind = wrap_offset(own_pos - before).astype(jnp.float32)
    tangent_raw = ahead_step + behind
    entries = 3 * own_pos.shape[1]
    tangent = (
        tangent_raw * lax.rsqrt(jnp.mean(tangent_raw * tangent_raw) + epsilon) / math.sqrt(entries)
    )
    length_ahead = jnp.sqrt(entries * (jnp.mean(ahead_step * ahead_step) + epsilon))
    length_behind = jnp.sqrt(entries * (jnp.mean(behind * behind) + epsilon))
    along_path = jnp.sum(force * tangent)
    band_push = (
        force - along_path * tangent + spring_constant * (length_ahead - length_behind) * tangent
    )
    return (band_push, along_path)


def body(coefficients, rotation, positions, start_pos, end_pos, species, depth):
    coeff_all = coefficients[0]
    planes = coeff_all.shape[1]
    flat_all = coeff_all.reshape(BANDS, -1)
    orbitals = jnp.einsum("ib,ik->bk", rotation[0], flat_all, preferred_element_type=jnp.float32)
    orbitals = orbitals.astype(jnp.bfloat16).reshape(BLOCK, planes, W * 2 * W)
    kind_ids = jnp.arange(SPECIES, dtype=jnp.int32)
    strength = jnp.sum(jnp.where(species[:, None] == kind_ids[None, :], depth[None, :], 0.0), 1)
    own_pos = positions[0]
    natural = jnp.arange(W, dtype=jnp.int32)
    table_f = forward_table(natural, W, G)
    table_i = inverse_table(natural, W, G)
    whole_vectors = lax.all_to_all(
        orbitals, ("band", "pw"), split_axis=0, concat_axis=1, tiled=True
    )
    spread = section_zy(whole_vectors, table_f, table_f)
    weighted, force_part = space_work(section_x(spread, table_f), own_pos, strength, G)
    partial_apply = section_zy_inverse(section_x_inverse(weighted, table_i), table_i, table_i)
    applied = lax.all_to_all(partial_apply, ("band", "pw"), split_axis=1, concat_axis=0, tiled=True)
    x_cells = lax.axis_index(("band", "pw")) * planes + jnp.arange(planes, dtype=jnp.int32)
    kinetic = kinetic_table(x_cells)
    orbitals_wide = orbitals.astype(jnp.float32)
    hamiltonian = kinetic[None] * orbitals_wide + applied
    numerator = jnp.sum(orbitals_wide * hamiltonian, axis=(1, 2))
    denominator = jnp.sum(orbitals_wide * orbitals_wide, axis=(1, 2))
    numerator, denominator, atom_force = lax.psum(
        (numerator, denominator, force_part), ("band", "pw")
    )
    npw_total = W * W * W
    ritz_values = numerator / npw_total / (denominator / npw_total + epsilon)
    residual = hamiltonian - ritz_values[:, None, None] * orbitals_wide
    search = (residual / (1.0 + kinetic)[None]).astype(jnp.bfloat16)
    search_pair = jnp.concatenate(
        [search.reshape(BLOCK, -1), (-rotate_quarter(search)).reshape(BLOCK, -1)], 0
    )
    intersections = (
        jnp.einsum("ik,jk->ij", flat_all, search_pair, preferred_element_type=jnp.float32)
        / npw_total
    )
    intersections = lax.psum(intersections, ("band", "pw")).astype(jnp.bfloat16)
    projected = jnp.einsum("ij,ik->jk", intersections, flat_all, preferred_element_type=jnp.float32)
    projection = projected[:BLOCK].reshape(BLOCK, planes, -1) + rotate_quarter(
        projected[BLOCK:].reshape(BLOCK, planes, -1)
    )
    correction = (search.astype(jnp.float32) - projection).astype(jnp.bfloat16)
    image_idx = lax.axis_index("img")
    before = passed_along(own_pos, "img", 1)
    after = passed_along(own_pos, "img", -1)
    before = jnp.where(image_idx == 0, start_pos, before)
    after = jnp.where(image_idx == lax.axis_size("img") - 1, end_pos, after)
    band_push, along_path = chain_forces(atom_force, own_pos, before, after)
    return (correction[None], ritz_values[None], band_push[None], along_path[None])


def solution(mesh):
    in_specs = (
        P("img", None, ("band", "pw"), None),
        P("img", None, None),
        P("img", None, None),
        P(),
        P(),
        P(),
        P(),
    )
    out_specs = (
        P("img", None, ("band", "pw"), None),
        P("img", None),
        P("img", None, None),
        P("img"),
    )
    return jax.shard_map(body, mesh=mesh, in_specs=in_specs, out_specs=out_specs, check_vma=False)
```

profile of v0, /device:TPU:0, one launch (start us, length us, event | category | flops | bytes accessed | tf_op | source)
XLA Modules:
  0.0 592.1 jit_solution(8768601264481166253)
XLA Ops:
  0.6 0.0 copy-start
  0.6 12.1 %copy.141 = bf16[128,8,2,2048]{3,1,2,0:T(8,128)(2,1)} copy(bf16[128,8,2,2048]{3,2,1,0:T(2,128)(2,1)} %bitcast.208) | data formatting | bytes 16777216
  12.7 5.8 convolution_convert_fusion
  18.5 2.8 reshape.676
  21.3 8.6 %all-to-all-start = ((bf16[256,2,2048]{2,1,0:T(2,128)(2,1)}), bf16[256,2,2048]{2,1,0:T(2,128)(2,1)}, u32[]{:S(2)}, u32[]{:S(2)}) async-start(bf16[256,2,2048]{2,1,0:T(2,128)(2,1)} %reshape.676), calls=%async_computation | async-start | bytes 4194304 | tf_op jit(solution)/shard_map/all_to_all | solution.py:189
  29.9 0.2 fusion.111
  30.1 0.2 negate_convert_fusion.1
  30.3 0.1 select_reduce_fusion
  30.4 0.1 fusion.79
  30.5 7.5 %fusion.29 = f32[64,64,64]{2,0,1:T(8,128)} fusion(f32[256,64]{0,1:T(8,128)S(1)} %get-tuple-element.67, f32[256,64]{0,1:T(8,128)S(1)} %get-tuple-element.74, s32[256]{0:T(256)S(1)} %bitcast.217, f32[256]{0:T(256)S(1)} %select_reduce_fusion), kind=kOutput, calls=%fused_computation.35 | convolution fusion | flops 806666240 | bytes 1181696 | tf_op jit(solution)/shard_map/dot_general | solution.py:114
  37.9 35.0 %all-to-all-done = bf16[256,2,2048]{2,1,0:T(2,128)(2,1)} async-done(((bf16[256,2,2048]{2,1,0:T(2,128)(2,1)}), bf16[256,2,2048]{2,1,0:T(2,128)(2,1)}, u32[]{:S(2)}, u32[]{:S(2)}) %all-to-all-start) | async-done | bytes 2097184 | tf_op jit(solution)/shard_map/all_to_all | solution.py:189
  72.9 2.5 copy.101
  75.4 1.5 copy.102
  76.9 17.9 %reshape.677 = bf16[16,32,32,2,32]{4,3,2,0,1:T(2,128)(2,1)} reshape(bf16[16,16,2,2048]{3,0,2,1:T(8,128)(2,1)} %copy.102) | data formatting | bytes 4194304 | tf_op jit(solution)/shard_map/reshape | solution.py:56
  94.8 12.6 %fusion.20 = bf16[16,32,64,2,64]{4,2,1,0,3:T(8,128)(2,1)} fusion(bf16[16,32,32,2,32,1]{4,3,2,0,1,5:T(2,128)(2,1)} %bitcast.203, bf16[1,32,2,64]{3,1,0,2:T(8,128)(2,1)S(1)} %get-tuple-element.57, bf16[1,32,2,64]{3,1,0,2:T(8,128)(2,1)S(1)} %get-tuple-element.56), kind=kOutput, calls=%fused_computation.24 | convolution fusion | flops 811663360 | bytes 10502144 | tf_op jit(solution)/shard_map/blycz,cydm->blmdz/dot_general | solution.py:60
  107.4 28.7 %fusion.1 = (f32[64,64,64]{2,0,1:T(8,128)}, bf16[16,64,64,2,64]{4,1,2,0,3:T(8,128)(2,1)}) fusion(f32[64,64,64]{2,0,1:T(8,128)} %fusion.29, bf16[16,32,64,2,64]{4,2,1,0,3:T(8,128)(2,1)} %fusion.20, bf16[1,32,2,64]{3,1,0,2:T(8,128)(2,1)S(1)} %get-tuple-element.57, bf16[1,32,2,64]{3,1,0,2:T(8,128)(2,1)S(1)} %get-tuple-element.56), kind=kOutput, calls=%fused_computation.3 | convolution fusion | flops 1107066880 | bytes 27279360 | tf_op jit(solution)/shard_map/bxycz,cxdn->bnydz/dot_general | solution.py:70
  136.1 18.9 %fusion.6 = bf16[16,32,64,2,64,1]{4,1,2,0,3,5:T(8,128)(2,1)} fusion(bf16[16,64,64,2,64]{4,1,2,0,3:T(8,128)(2,1)} %get-tuple-element.40, bf16[1,64,2,32]{1,3,0,2:T(8,128)(2,1)S(1)} %get-tuple-element.55, bf16[1,64,2,32]{1,3,0,2:T(8,128)(2,1)S(1)} %get-tuple-element.54), kind=kOutput, calls=%fused_computation.10 | convolution fusion | flops 1077968896 | bytes 25182208 | tf_op jit(solution)/shard_map/bnydz,dncx->bxycz/dot_general | solution.py:76
  155.0 19.3 %convolution_bitcast_fusion = f32[16,32,32,2,32]{4,2,3,1,0:T(8,128)} fusion(bf16[16,32,64,2,64,1]{4,1,2,0,3,5:T(8,128)(2,1)} %fusion.6, bf16[1,64,2,32]{1,3,0,2:T(8,128)(2,1)S(1)} %get-tuple-element.55, bf16[1,64,2,32]{1,3,0,2:T(8,128)(2,1)S(1)} %get-tuple-element.54), kind=kOutput, calls=%fused_computation.25 | convolution fusion | flops 807469056 | bytes 12599296 | tf_op jit(solution)/shard_map/blydn,dnck->blyck/dot_general | solution.py:89
  174.3 28.6 %copy.138 = f32[16,32,32,2,32]{4,3,2,0,1:T(2,128)} copy(f32[16,32,32,2,32]{4,2,3,1,0:T(8,128)} %convolution_bitcast_fusion) | data formatting | bytes 8388608 | tf_op jit(solution)/shard_map/reshape | solution.py:90
  202.9 21.7 %reshape.699 = f32[16,32,2048]{2,0,1:T(8,128)} reshape(f32[16,32,32,2,32]{4,3,2,0,1:T(2,128)} %copy.138) | data formatting | bytes 8388608 | tf_op jit(solution)/shard_map/reshape | solution.py:90
  224.6 10.1 %all-to-all-start.1 = ((f32[16,32,2048]{2,0,1:T(8,128)}), f32[16,32,2048]{2,0,1:T(8,128)}, u32[]{:S(2)}, u32[]{:S(2)}) async-start(f32[16,32,2048]{2,0,1:T(8,128)} %reshape.699), calls=%async_computation.1 | async-start | bytes 8388608 | tf_op jit(solution)/shard_map/all_to_all | solution.py:195
  234.7 1.3 collective-permute-start
  236.0 3.0 collective-permute-start.1
  239.1 0.1 fusion.83
  239.2 0.1 convert_multiply_fusion.4
  239.3 0.1 convert_multiply_fusion.6
  239.4 5.0 broadcast_multiply_fusion.2
  244.4 0.1 add.348
  244.5 3.0 copy.112
  247.5 5.1 reshape.682
  252.7 0.6 multiply_reduce_fusion.3
  254.0 0.6 multiply_reduce_fusion
  256.0 1.8 broadcast_multiply_fusion.4
  257.8 2.5 copy.119
  260.3 3.1 div.129
  263.4 12.6 %fusion.14 = f32[64,768]{1,0:T(8,128)S(1)} fusion(f32[64,4096]{1,0:T(8,128)} %div.129, f32[256,4096]{0,1:T(8,128)} %bitcast.212, f32[256,4096]{0,1:T(8,128)} %bitcast.213, f32[256,4096]{0,1:T(8,128)} %bitcast.211), kind=kOutput, calls=%fused_computation.18 | convolution fusion | flops 2422210560 | bytes 13828096 | tf_op jit(solution)/shard_map/dot_general | solution.py:124
  276.1 0.1 fusion.75
  276.2 36.9 %all-to-all-done.1 = f32[16,32,2048]{2,0,1:T(8,128)} async-done(((f32[16,32,2048]{2,0,1:T(8,128)}), f32[16,32,2048]{2,0,1:T(8,128)}, u32[]{:S(2)}, u32[]{:S(2)}) %all-to-all-start.1) | async-done | bytes 4194336 | tf_op jit(solution)/shard_map/all_to_all | solution.py:195
  313.0 5.5 copy.110
  318.5 4.7 copy.109
  323.2 5.9 %copy.143 = f32[32,8,2,2048]{3,1,2,0:T(8,128)} copy(f32[32,8,2,2048]{3,2,1,0:T(2,128)S(1)} %bitcast.206) | data formatting | bytes 8388608
  329.1 18.0 %all_to_all.36 = f32[256,2,32,2,32]{4,3,2,0,1:T(2,128)} reshape(f32[16,16,2,2048]{3,1,0,2:T(8,128)} %copy.109) | data formatting | bytes 8388608 | tf_op jit(solution)/shard_map/all_to_all | solution.py:195
  347.1 20.8 %copy.114 = f32[256,2,32,2,32]{0,4,3,2,1:T(8,128)} copy(f32[256,2,32,2,32]{4,3,2,0,1:T(2,128)} %all_to_all.36) | data formatting | bytes 8388608 | tf_op jit(solution)/shard_map/all_to_all | solution.py:195
  367.9 3.3 fusion.37
  371.1 54.3 %all-reduce.1 = (f32[256]{0:T(256)S(1)}, f32[256]{0:T(256)S(1)}) all-reduce(f32[256]{0:T(256)S(1)} %get-tuple-element.25, f32[256]{0:T(256)S(1)} %get-tuple-element.24), channel_id=1, replica_groups=mesh['img'=2,'band'=4,'pw'=4] {'band','pw'}, use_global_device_ids=true, to_apply=%region_4.5 | all-reduce | flops 512 | bytes 4096 | tf_op jit(solution)/shard_map/psum | solution.py:202
  425.5 4.6 fusion.41
  430.2 0.8 copy-done.3
  431.0 1.5 divide_convert_fusion
  432.5 0.1 slice_negate_fusion.1
  432.6 0.2 maximum_negate_fusion
  432.8 2.9 copy.115
  435.7 8.2 %multiply_bitcast_fusion = f32[1024,512]{0,1:T(8,128)S(1)} fusion(bf16[1024,4096]{1,0:T(8,128)(2,1)} %bitcast.199, bf16[256,4096]{1,0:T(8,128)(2,1)} %copy.115, bf16[256,4096]{1,0:T(8,128)(2,1)} %fusion.41), kind=kOutput, calls=%fused_computation.59 | convolution fusion | flops 4303880192 | bytes 14680064 | tf_op jit(solution)/shard_map/ik,jk->ij/dot_general | solution.py:213
  444.0 97.9 %all-reduce.3 = (bf16[1024,512]{0,1:T(8,128)(2,1)}, f32[3,256]{1,0:T(4,128)S(1)}) all-reduce(f32[1024,512]{0,1:T(8,128)S(1)} %multiply_bitcast_fusion, f32[3,256]{1,0:T(4,128)S(1)} %pad_maximum_fusion.9), channel_id=1, replica_groups=mesh['img'=2,'band'=4,'pw'=4] {'band','pw'}, use_global_device_ids=true, to_apply=%region_5.6 | all-reduce | flops 525056 | bytes 3151872 | tf_op jit(solution)/shard_map/psum | solution.py:216
  541.8 0.6 multiply_reduce_fusion.2
  543.1 0.6 broadcast_in_dim.21
  543.7 7.2 %fusion.152 = f32[512,4096]{1,0:T(8,128)S(1)} fusion(bf16[1024,512]{0,1:T(8,128)(2,1)} %get-tuple-element.29, bf16[1024,4096]{1,0:T(8,128)(2,1)} %bitcast.200), kind=kOutput, calls=%fused_computation.217 | convolution fusion | flops 4294967296 | bytes 17825792 | tf_op jit(solution)/shard_map/ij,ik->jk/dot_general | solution.py:217
  550.9 3.8 fusion.146
  554.6 5.6 copy.116
  560.2 2.8 slice_negate_fusion
  563.0 2.4 pad_maximum_fusion
  565.5 5.4 copy.118
  570.9 6.6 %reshape.680 = f32[1,256,2,2048]{3,2,1,0:T(2,128)} reshape(f32[256,4096]{1,0:T(8,128)} %get-tuple-element.41) | data formatting | bytes 8388608 | tf_op jit(solution)/shard_map/reshape | solution.py:218
  577.4 10.7 %fusion.35 = bf16[1,256,2,2048]{3,1,2,0:T(8,128)(2,1)S(1)} fusion(f32[1,256,2,2048]{3,1,2,0:T(8,128)} %copy.118, f32[1,256,2,2048]{3,2,1,0:T(2,128)} %reshape.680, f32[16,16,2,2048]{3,1,0,2:T(8,128)} %copy.109, f32[1,256,2,2048]{3,2,1,0:T(2,128)} %reshape.682, f32[2,2048]{1,0:T(2,128)S(1)} %get-tuple-element.53, f32[256]{0:T(256)S(1)} %add_divide_fusion, ...), kind=kLoop, calls=%fused_computation.43 | loop fusion | flops 10485760 | bytes 18908160 | tf_op jit(solution)/shard_map/convert_element_type | solution.py:221
  588.1 3.5 copy.120
  (34 shorter events, 0.1 us)
Async XLA Ops:
  0.6 12.1 %copy-start = (bf16[1,1024,256]{2,1,0:T(8,128)(2,1)S(1)}, bf16[1,1024,256]{2,1,0:T(8,128)(2,1)}, u32[]{:S(2)}) copy-start(bf16[1,1024,256]{2,1,0:T(8,128)(2,1)} %param.8) | copy-start | bytes 1572868
  18.5 11.8 %copy-start.8 = (s32[256]{0:T(256)S(1)}, s32[256]{0:T(256)}, u32[]{:S(2)}) copy-start(s32[256]{0:T(256)} %param.12) | copy-start | bytes 3076
  18.5 11.8 %copy-start.9 = (f32[4]{0:T(128)S(1)}, f32[4]{0:T(128)}, u32[]{:S(2)}) copy-start(f32[4]{0:T(128)} %param.13) | copy-start | bytes 52
  18.5 11.9 %copy-start.4 = (s32[1,3,256]{2,0,1:T(1,128)S(1)}, s32[1,3,256]{2,0,1:T(1,128)}, u32[]{:S(2)}) copy-start(s32[1,3,256]{2,0,1:T(1,128)} %param.9) | copy-start | bytes 9220
  21.3 51.6 %all-to-all-start = ((bf16[256,2,2048]{2,1,0:T(2,128)(2,1)}), bf16[256,2,2048]{2,1,0:T(2,128)(2,1)}, u32[]{:S(2)}, u32[]{:S(2)}) async-start(bf16[256,2,2048]{2,1,0:T(2,128)(2,1)} %reshape.676), calls=%async_computation | async-start | bytes 4194304 | tf_op jit(solution)/shard_map/all_to_all | solution.py:189
  224.6 88.5 %all-to-all-start.1 = ((f32[16,32,2048]{2,0,1:T(8,128)}), f32[16,32,2048]{2,0,1:T(8,128)}, u32[]{:S(2)}, u32[]{:S(2)}) async-start(f32[16,32,2048]{2,0,1:T(8,128)} %reshape.699), calls=%async_computation.1 | async-start | bytes 8388608 | tf_op jit(solution)/shard_map/all_to_all | solution.py:195
  234.7 18.0 %collective-permute-start = (s32[3,256]{1,0:T(4,128)S(1)}, s32[3,256]{1,0:T(4,128)S(1)}, u32[]{:S(2)}, u32[]{:S(2)}) collective-permute-start(s32[3,256]{1,0:T(4,128)S(1)} %bitcast.224), channel_id=1, source_target_pairs={{16,0},{17,1},{18,2},{19,3},{20,4},{21,5},{22,6},{23,7},{24,8},{25... | collective-permute-start | bytes 9224 | tf_op jit(solution)/shard_map/ppermute | solution.py:22
  236.0 16.7 %collective-permute-start.1 = (s32[3,256]{1,0:T(4,128)S(1)}, s32[3,256]{1,0:T(4,128)S(1)}, u32[]{:S(2)}, u32[]{:S(2)}) collective-permute-start(s32[3,256]{1,0:T(4,128)S(1)} %bitcast.225), channel_id=1, source_target_pairs={{0,16},{1,17},{2,18},{3,19},{4,20},{5,21},{6,22},{7,23},{8,24},{9,... | collective-permute-start | bytes 9224 | tf_op jit(solution)/shard_map/ppermute | solution.py:22
  247.5 5.2 copy-start.6
  247.5 5.2 copy-start.7
  425.5 151.9 %copy-start.5 = (f32[256]{0:T(256)}, f32[256]{0:T(256)S(1)}, u32[]{:S(2)}) copy-start(f32[256]{0:T(256)S(1)} %add_divide_fusion) | copy-start | bytes 3076
  425.5 4.7 copy-start.2
  425.5 5.5 copy-start.3
  577.4 14.2 %copy-start.1 = (bf16[1,1024,256]{2,1,0:T(8,128)(2,1)S(1)}, bf16[1,1024,256]{2,1,0:T(8,128)(2,1)}, u32[]{:S(2)}) copy-start(bf16[1,1024,256]{2,1,0:T(8,128)(2,1)} %param.8) | copy-start | bytes 1572868
where the time goes:
time: 600 us; the launch traced here: 592 us
  local copies, waits for them, and re-layouts  185 us (31%)
  blocking collectives  152 us (25%)
  matrix products  121 us (20%)
  waiting for transfers between devices  71.8 us (12%)
  other arithmetic  35.2 us (6%)
  starting transfers between devices  23 us (4%)
    psum x1, blocking collectives, body(): intersections = lax.psum(intersections, ('band', 'pw')).astype(jnp.bfloat16)  97.9 us
    psum x1, blocking collectives, body(): lax.psum((numerator, denominator, force_part), ('band', 'pw'))  54.3 us
    reshape x2, local copies, waits for them, and re-layouts, section_zy_inverse(): return along_z.reshape(leading, planes, W * 2 * W)  50.3 us
    all_to_all x4, local copies, waits for them, and re-layouts, body(): lax.all_to_all(partial_apply, ('band', 'pw'), split_axis=1, concat_axis=0...  48.9 us
    all_to_all x1, waiting for transfers between devices, body(): lax.all_to_all(partial_apply, ('band', 'pw'), split_axis=1, concat_axis=0...  36.9 us
    all_to_all x1, waiting for transfers between devices, body(): lax.all_to_all(orbitals, ('band', 'pw'), split_axis=0, concat_axis=1, til...  35 us
    dot_general x1, matrix products, section_x(): jnp.einsum('bxycz,cxdn->bnydz', split_up, table_x, preferred_element_type...  28.7 us
    unnamed x26, local copies, waits for them, and re-layouts  22.4 us
  transfers between devices with their start and end apart: 4, of which 2 were waited for; matrix products, arithmetic and copies ran while one was open for 7% of the time, Pallas kernels for 0%

commit v1 on v0

--- a/solution.py
+++ b/solution.py
@@ -192,7 +192,15 @@
     spread = section_zy(whole_vectors, table_f, table_f)
     weighted, force_part = space_work(section_x(spread, table_f), own_pos, strength, G)
     partial_apply = section_zy_inverse(section_x_inverse(weighted, table_i), table_i, table_i)
-    applied = lax.all_to_all(partial_apply, ("band", "pw"), split_axis=1, concat_axis=0, tiled=True)
+    applied = jnp.concatenate(
+        lax.all_to_all(
+            jnp.stack(jnp.split(partial_apply, lax.axis_size(("band", "pw")), axis=1)),
+            ("band", "pw"),
+            0,
+            0,
+        ),
+        axis=0,
+    )
     x_cells = lax.axis_index(("band", "pw")) * planes + jnp.arange(planes, dtype=jnp.int32)
     kinetic = kinetic_table(x_cells)
     orbitals_wide = orbitals.astype(jnp.float32)

time: 600 us -> 639 us (1.065)
  local copies, waits for them, and re-layouts: 185 us -> 209 us
  matrix products: 121 us -> 136 us
    all_to_all x4 -> x0, local copies, waits for them, and re-layouts: 48.9 us -> none  [body(): lax.all_to_all(partial_apply, ('band', 'pw'), split_axis=1, concat_axis=0...]
    reshape x1 -> x3, local copies, waits for them, and re-layouts: 5.4 us -> 46.9 us  [body(): jnp.concatenate(lax.all_to_all(jnp.stack(jnp.split(partial_apply, lax.axi...]
    unnamed x26 -> x45, local copies, waits for them, and re-layouts: 22.4 us -> 57.7 us
    reshape x2 -> x1, local copies, waits for them, and re-layouts: 50.3 us -> 21.7 us  [section_zy_inverse(): return along_z.reshape(leading, planes, W * 2 * W)]
    dot_general x0 -> x1, local copies, waits for them, and re-layouts: none -> 28.5 us  [section_zy_inverse(): jnp.einsum('blydn,dnck->blyck', along_y, table_z, preferred_element_type=...]
    dot_general x1, matrix products: 28.7 us -> 43.8 us  [section_x(): jnp.einsum('bxycz,cxdn->bnydz', split_up, table_x, preferred_element_type...]
    convert_element_type x1, other arithmetic: 10.7 us -> 3.87 us  [body(): correction = (search.astype(jnp.float32) - projection).astype(jnp.bfloat16)]
  transfers between devices with their start and end apart: 4 -> 4, of which waited for: 2 -> 2; matrix products, arithmetic and copies ran while one was open for 7% -> 6% of each run, Pallas kernels for 0% -> 0%
where the time goes in v1:
time: 639 us; the launch traced here: 630 us
  local copies, waits for them, and re-layouts  209 us (33%)
  blocking collectives  152 us (24%)
  matrix products  136 us (21%)
  waiting for transfers between devices  76.7 us (12%)
  other arithmetic  29.6 us (5%)
  starting transfers between devices  23.3 us (4%)
    psum x1, blocking collectives, body(): intersections = lax.psum(intersections, ('band', 'pw')).astype(jnp.bfloat16)  97.9 us
    unnamed x45, local copies, waits for them, and re-layouts  57.7 us
    psum x1, blocking collectives, body(): lax.psum((numerator, denominator, force_part), ('band', 'pw'))  54.3 us
    reshape x3, local copies, waits for them, and re-layouts, body(): jnp.concatenate(lax.all_to_all(jnp.stack(jnp.split(partial_apply, lax.axi...  46.9 us
    dot_general x1, matrix products, section_x(): jnp.einsum('bxycz,cxdn->bnydz', split_up, table_x, preferred_element_type...  43.8 us
    all_to_all x1, waiting for transfers between devices, body(): lax.all_to_all(jnp.stack(jnp.split(partial_apply, lax.axis_size(('band',...  41.7 us
    all_to_all x1, waiting for transfers between devices, body(): lax.all_to_all(orbitals, ('band', 'pw'), split_axis=0, concat_axis=1, til...  35 us
    dot_general x1, local copies, waits for them, and re-layouts, section_zy_inverse(): jnp.einsum('blydn,dnck->blyck', along_y, table_z, preferred_element_type=...  28.5 us
  transfers between devices with their start and end apart: 4, of which 2 were waited for; matrix products, arithmetic and copies ran while one was open for 6% of the time, Pallas kernels for 0%

profile of v1, /device:TPU:0, one launch (start us, length us, event | category | flops | bytes accessed | tf_op | source)
XLA Modules:
  0.0 630.4 jit_solution(16365451656591374133)
XLA Ops:
  0.6 12.1 %copy.130 = bf16[128,8,2,2048]{3,1,2,0:T(8,128)(2,1)} copy(bf16[128,8,2,2048]{3,2,1,0:T(2,128)(2,1)} %bitcast.257) | data formatting | bytes 16777216
  12.7 5.8 convolution_convert_fusion
  18.5 2.8 reshape.683
  21.3 8.8 %all-to-all-start = ((bf16[256,2,2048]{2,1,0:T(2,128)(2,1)}), bf16[256,2,2048]{2,1,0:T(2,128)(2,1)}, u32[]{:S(2)}, u32[]{:S(2)}) async-start(bf16[256,2,2048]{2,1,0:T(2,128)(2,1)} %reshape.683), calls=%async_computation | async-start | bytes 4194304 | tf_op jit(solution)/shard_map/all_to_all | solution.py:189
  30.7 7.5 %fusion.29 = f32[64,64,64]{2,0,1:T(8,128)} fusion(f32[256,64]{0,1:T(8,128)S(1)} %get-tuple-element.67, f32[256,64]{0,1:T(8,128)S(1)} %get-tuple-element.74, s32[256]{0:T(256)S(1)} %bitcast.266, f32[256]{0:T(256)S(1)} %select_reduce_fusion), kind=kOutput, calls=%fused_computation.35 | convolution fusion | flops 806666240 | bytes 1181696 | tf_op jit(solution)/shard_map/dot_general | solution.py:114
  38.2 35.0 %all-to-all-done = bf16[256,2,2048]{2,1,0:T(2,128)(2,1)} async-done(((bf16[256,2,2048]{2,1,0:T(2,128)(2,1)}), bf16[256,2,2048]{2,1,0:T(2,128)(2,1)}, u32[]{:S(2)}, u32[]{:S(2)}) %all-to-all-start) | async-done | bytes 2097184 | tf_op jit(solution)/shard_map/all_to_all | solution.py:189
  73.2 2.5 copy.91
  75.6 1.5 copy.92
  77.2 17.9 %reshape.684 = bf16[16,32,32,2,32]{4,3,2,0,1:T(2,128)(2,1)} reshape(bf16[16,16,2,2048]{3,0,2,1:T(8,128)(2,1)} %copy.92) | data formatting | bytes 4194304 | tf_op jit(solution)/shard_map/reshape | solution.py:56
  95.0 12.6 %fusion.20 = bf16[16,32,64,2,64]{4,2,1,0,3:T(8,128)(2,1)} fusion(bf16[16,32,32,2,32,1]{4,3,2,0,1,5:T(2,128)(2,1)} %bitcast.253, bf16[1,32,2,64]{3,1,0,2:T(8,128)(2,1)S(1)} %get-tuple-element.57, bf16[1,32,2,64]{3,1,0,2:T(8,128)(2,1)S(1)} %get-tuple-element.56), kind=kOutput, calls=%fused_computation.24 | convolution fusion | flops 811663360 | bytes 10502144 | tf_op jit(solution)/shard_map/blycz,cydm->blmdz/dot_general | solution.py:60
  107.7 43.8 %fusion.1 = (f32[64,64,64]{2,0,1:T(8,128)}, bf16[16,64,64,2,64]{4,1,2,0,3:T(8,128)(2,1)}) fusion(f32[64,64,64]{2,0,1:T(8,128)} %fusion.29, bf16[16,32,64,2,64]{4,2,1,0,3:T(8,128)(2,1)} %fusion.20, bf16[1,32,2,64]{3,1,0,2:T(8,128)(2,1)S(1)} %get-tuple-element.57, bf16[1,32,2,64]{3,1,0,2:T(8,128)(2,1)S(1)} %get-tuple-element.56), kind=kOutput, calls=%fused_computation.3 | convolution fusion | flops 1107066880 | bytes 27279360 | tf_op jit(solution)/shard_map/bxycz,cxdn->bnydz/dot_general | solution.py:70
  151.5 19.0 %fusion.6 = bf16[16,32,64,2,64,1]{4,1,2,0,3,5:T(8,128)(2,1)} fusion(bf16[16,64,64,2,64]{4,1,2,0,3:T(8,128)(2,1)} %get-tuple-element.40, bf16[1,64,2,32]{1,3,0,2:T(8,128)(2,1)S(1)} %get-tuple-element.55, bf16[1,64,2,32]{1,3,0,2:T(8,128)(2,1)S(1)} %get-tuple-element.54), kind=kOutput, calls=%fused_computation.10 | convolution fusion | flops 1077968896 | bytes 25182208 | tf_op jit(solution)/shard_map/bnydz,dncx->bxycz/dot_general | solution.py:76
  170.5 19.3 %convolution_bitcast_fusion = f32[16,32,32,2,32]{4,2,3,1,0:T(8,128)} fusion(bf16[16,32,64,2,64,1]{4,1,2,0,3,5:T(8,128)(2,1)} %fusion.6, bf16[1,64,2,32]{1,3,0,2:T(8,128)(2,1)S(1)} %get-tuple-element.55, bf16[1,64,2,32]{1,3,0,2:T(8,128)(2,1)S(1)} %get-tuple-element.54), kind=kOutput, calls=%fused_computation.25 | convolution fusion | flops 807469056 | bytes 12599296 | tf_op jit(solution)/shard_map/blydn,dnck->blyck/dot_general | solution.py:89
  189.7 28.5 %copy.97 = f32[16,32,32,2,32]{4,3,2,1,0:T(2,128)} copy(f32[16,32,32,2,32]{4,2,3,1,0:T(8,128)} %convolution_bitcast_fusion) | data formatting | bytes 8388608 | tf_op jit(solution)/shard_map/blydn,dnck->blyck/dot_general | solution.py:89
  218.2 21.7 %reshape.686 = f32[16,32,2048]{2,1,0:T(8,128)} reshape(f32[16,32,32,2,32]{4,3,2,1,0:T(2,128)} %copy.97) | data formatting | bytes 8388608 | tf_op jit(solution)/shard_map/reshape | solution.py:90
  239.9 2.0 fusion.65
  241.9 2.1 fusion.64
  244.0 2.1 fusion.63
  246.1 2.1 fusion.62
  248.2 2.0 fusion.61
  250.2 2.1 fusion.60
  252.2 2.1 fusion.59
  254.3 2.1 fusion.58
  256.4 2.0 fusion.57
  258.4 2.1 fusion.56
  260.5 2.1 fusion.55
  262.6 2.1 fusion.54
  264.7 2.0 fusion.53
  266.7 2.1 fusion.52
  268.8 2.1 fusion.51
  270.8 2.1 fusion.50
  272.9 10.1 %all-to-all-start.1 = ((f32[16,16,2,2048]{3,2,1,0:T(2,128)}), f32[16,16,2,2048]{3,2,1,0:T(2,128)}, u32[]{:S(2)}, u32[]{:S(2)}) async-start(f32[16,16,2,2048]{3,2,1,0:T(2,128)} %fusion.50), calls=%async_computation.1 | async-start | bytes 8388608 | tf_op jit(solution)/shard_map/all_to_all | solution.py:196
  283.1 1.3 collective-permute-start
  284.4 3.0 collective-permute-start.1
  287.8 5.1 broadcast_multiply_fusion.2
  293.0 3.0 copy.128
  296.0 0.6 multiply_reduce_fusion.3
  299.3 1.8 broadcast_multiply_fusion.4
  301.0 2.5 copy.106
  303.6 3.4 div.129
  306.9 12.6 %fusion.14 = f32[64,768]{1,0:T(8,128)S(1)} fusion(f32[64,4096]{1,0:T(8,128)} %div.129, f32[256,4096]{0,1:T(8,128)} %bitcast.261, f32[256,4096]{0,1:T(8,128)} %bitcast.262, f32[256,4096]{0,1:T(8,128)} %bitcast.260), kind=kOutput, calls=%fused_computation.18 | convolution fusion | flops 2422210560 | bytes 13828096 | tf_op jit(solution)/shard_map/dot_general | solution.py:124
  319.7 41.7 %all-to-all-done.1 = f32[16,16,2,2048]{3,2,1,0:T(2,128)} async-done(((f32[16,16,2,2048]{3,2,1,0:T(2,128)}), f32[16,16,2,2048]{3,2,1,0:T(2,128)}, u32[]{:S(2)}, u32[]{:S(2)}) %all-to-all-start.1) | async-done | bytes 4194336 | tf_op jit(solution)/shard_map/all_to_all | solution.py:196
  361.4 8.0 %copy.132 = f32[32,8,2,2048]{3,1,2,0:T(8,128)} copy(f32[32,8,2,2048]{3,2,1,0:T(2,128)} %bitcast.101) | data formatting | bytes 8388608
  369.3 18.8 %reshape.709 = f32[256,2,32,2,32]{4,3,2,1,0:T(2,128)} reshape(f32[16,16,2,2048]{3,2,1,0:T(2,128)} %all-to-all-done.1) | data formatting | bytes 8388608 | tf_op jit(solution)/shard_map/reshape | solution.py:195
  388.1 20.8 %copy.102 = f32[256,2,32,2,32]{0,4,3,2,1:T(8,128)} copy(f32[256,2,32,2,32]{4,3,2,1,0:T(2,128)} %reshape.709) | data formatting | bytes 8388608 | tf_op jit(solution)/shard_map/reshape | solution.py:195
  408.9 3.3 fusion.32
  412.2 54.3 %all-reduce.1 = (f32[256]{0:T(256)S(1)}, f32[256]{0:T(256)S(1)}) all-reduce(f32[256]{0:T(256)S(1)} %get-tuple-element.25, f32[256]{0:T(256)S(1)} %get-tuple-element.24), channel_id=1, replica_groups=mesh['img'=2,'band'=4,'pw'=4] {'band','pw'}, use_global_device_ids=true, to_apply=%region_4.5 | all-reduce | flops 512 | bytes 4096 | tf_op jit(solution)/shard_map/psum | solution.py:210
  466.5 4.7 fusion.36
  471.2 0.8 copy-done.4
  472.0 1.5 divide_convert_fusion
  473.9 2.9 copy.103
  476.7 8.2 %multiply_bitcast_fusion = f32[1024,512]{0,1:T(8,128)S(1)} fusion(bf16[1024,4096]{1,0:T(8,128)(2,1)} %bitcast.247, bf16[256,4096]{1,0:T(8,128)(2,1)} %copy.103, bf16[256,4096]{1,0:T(8,128)(2,1)} %fusion.36), kind=kOutput, calls=%fused_computation.54 | convolution fusion | flops 4303880192 | bytes 14680064 | tf_op jit(solution)/shard_map/ik,jk->ij/dot_general | solution.py:221
  485.0 97.9 %all-reduce.3 = (bf16[1024,512]{0,1:T(8,128)(2,1)}, f32[3,256]{1,0:T(4,128)S(1)}) all-reduce(f32[1024,512]{0,1:T(8,128)S(1)} %multiply_bitcast_fusion, f32[3,256]{1,0:T(4,128)S(1)} %pad_maximum_fusion.9), channel_id=1, replica_groups=mesh['img'=2,'band'=4,'pw'=4] {'band','pw'}, use_global_device_ids=true, to_apply=%region_5.6 | all-reduce | flops 525056 | bytes 3151872 | tf_op jit(solution)/shard_map/psum | solution.py:224
  584.8 7.2 %fusion.163 = f32[512,4096]{1,0:T(8,128)S(1)} fusion(bf16[1024,512]{0,1:T(8,128)(2,1)} %get-tuple-element.29, bf16[1024,4096]{1,0:T(8,128)(2,1)} %bitcast.248), kind=kOutput, calls=%fused_computation.244 | convolution fusion | flops 4294967296 | bytes 17825792 | tf_op jit(solution)/shard_map/ij,ik->jk/dot_general | solution.py:225
  592.0 3.7 fusion.157
  595.7 5.6 copy.104
  601.3 4.1 slice_negate_fusion
  605.4 5.6 copy.127
  611.0 7.2 %copy.98 = f32[1,256,2,2048]{1,3,2,0:T(8,128)} copy(f32[1,256,2,2048]{3,2,1,0:T(2,128)} %bitcast.62) | data formatting | bytes 8388608 | tf_op jit(solution)/shard_map/reshape | solution.py:195
  618.3 2.1 pad_maximum_fusion
  620.5 0.6 copy-done.3
  621.1 1.3 copy-done.5
  622.4 3.9 subtract_convert_fusion
  626.3 3.9 copy.107
  (51 shorter events, 3.3 us)
Async XLA Ops:
  0.6 12.1 %copy-start = (bf16[1,1024,256]{2,1,0:T(8,128)(2,1)S(1)}, bf16[1,1024,256]{2,1,0:T(8,128)(2,1)}, u32[]{:S(2)}) copy-start(bf16[1,1024,256]{2,1,0:T(8,128)(2,1)} %param.8) | copy-start | bytes 1572868
  18.5 12.0 %copy-start.10 = (s32[256]{0:T(256)S(1)}, s32[256]{0:T(256)}, u32[]{:S(2)}) copy-start(s32[256]{0:T(256)} %param.12) | copy-start | bytes 3076
  18.5 12.0 %copy-start.11 = (f32[4]{0:T(128)S(1)}, f32[4]{0:T(128)}, u32[]{:S(2)}) copy-start(f32[4]{0:T(128)} %param.13) | copy-start | bytes 52
  18.5 12.1 %copy-start.6 = (s32[1,3,256]{2,0,1:T(1,128)S(1)}, s32[1,3,256]{2,0,1:T(1,128)}, u32[]{:S(2)}) copy-start(s32[1,3,256]{2,0,1:T(1,128)} %param.9) | copy-start | bytes 9220
  21.3 51.8 %all-to-all-start = ((bf16[256,2,2048]{2,1,0:T(2,128)(2,1)}), bf16[256,2,2048]{2,1,0:T(2,128)(2,1)}, u32[]{:S(2)}, u32[]{:S(2)}) async-start(bf16[256,2,2048]{2,1,0:T(2,128)(2,1)} %reshape.683), calls=%async_computation | async-start | bytes 4194304 | tf_op jit(solution)/shard_map/all_to_all | solution.py:189
  272.9 88.4 %all-to-all-start.1 = ((f32[16,16,2,2048]{3,2,1,0:T(2,128)}), f32[16,16,2,2048]{3,2,1,0:T(2,128)}, u32[]{:S(2)}, u32[]{:S(2)}) async-start(f32[16,16,2,2048]{3,2,1,0:T(2,128)} %fusion.50), calls=%async_computation.1 | async-start | bytes 8388608 | tf_op jit(solution)/shard_map/all_to_all | solution.py:196
  283.1 12.9 %collective-permute-start = (s32[3,256]{1,0:T(4,128)S(1)}, s32[3,256]{1,0:T(4,128)S(1)}, u32[]{:S(2)}, u32[]{:S(2)}) collective-permute-start(s32[3,256]{1,0:T(4,128)S(1)} %bitcast.273), channel_id=1, source_target_pairs={{16,0},{17,1},{18,2},{19,3},{20,4},{21,5},{22,6},{23,7},{24,8},{25... | collective-permute-start | bytes 9224 | tf_op jit(solution)/shard_map/ppermute | solution.py:22
  284.4 11.6 %collective-permute-start.1 = (s32[3,256]{1,0:T(4,128)S(1)}, s32[3,256]{1,0:T(4,128)S(1)}, u32[]{:S(2)}, u32[]{:S(2)}) collective-permute-start(s32[3,256]{1,0:T(4,128)S(1)} %bitcast.274), channel_id=1, source_target_pairs={{0,16},{1,17},{2,18},{3,19},{4,20},{5,21},{6,22},{7,23},{8,24},{9,... | collective-permute-start | bytes 9224 | tf_op jit(solution)/shard_map/ppermute | solution.py:22
  292.9 3.1 copy-start.8
  292.9 3.1 copy-start.9
  466.5 153.9 %copy-start.7 = (f32[256]{0:T(256)}, f32[256]{0:T(256)S(1)}, u32[]{:S(2)}) copy-start(f32[256]{0:T(256)S(1)} %add_divide_fusion) | copy-start | bytes 3076
  466.5 4.7 copy-start.2
  466.5 5.5 copy-start.4
  618.3 2.8 copy-start.3
  618.3 4.1 copy-start.5
  622.4 7.8 %copy-start.1 = (bf16[1,1024,256]{2,1,0:T(8,128)(2,1)S(1)}, bf16[1,1024,256]{2,1,0:T(8,128)(2,1)}, u32[]{:S(2)}) copy-start(bf16[1,1024,256]{2,1,0:T(8,128)(2,1)} %param.8) | copy-start | bytes 1572868
